TPU v7x, 32 devices: a whole 2x2x4 slice. The times are simulated.
32 devices in a mesh: pb: 8 (over z, y), ka: 2 (over x), ha: 2 (over core).
Axes of the slice: x: 2, y: 2, z: 4, core: 2. Of those that a mesh axis runs over, the one named last changes fastest.
Arguments:
- queries: bfloat16 [8192, 256], P(('pb', 'ka'), 'ha'), may hold values from -130 to 130
- key_codes: int32 [8192, 256], P(('ka', 'pb'), 'ha'), may hold values from -127 to 127
- value_codes: int32 [8192, 256], P(('ka', 'pb'), 'ha'), may hold values from -127 to 127
- key_scale: float32 [], replicated, may hold values from 0.015 to 0.02
- value_scale: float32 [], replicated, may hold values from 0.01 to 0.02
- out_grad: bfloat16 [8192, 256], P(('pb', 'ka'), 'ha'), may hold values from -256 to 256
Outputs:
- query_grad: float32 [8192, 256], P(('pb', 'ka'), 'ha')
- key_grad: float32 [8192, 256], P(('ka', 'pb'), 'ha')
- value_grad: float32 [8192, 256], P(('ka', 'pb'), 'ha')
All inputs are finite; a program needn't handle non-finite values.
Results may differ from a plain program's by a relative error of at most 0.017.
Values may be sent and summed in bfloat16 or wider, within the bound.
A program may use at most 128 MiB of HBM per device.

v0:
```python
import math
import jax
import jax.numpy as jnp
from jax import lax
from jax.sharding import PartitionSpec as P


def merged(part, axis, combine):
    gathered = jax.tree.map(lambda a: lax.all_gather(a, axis), part)

    def take(source):
        return jax.tree.map(lambda a: lax.dynamic_index_in_dim(a, source, 0, False), gathered)

    return lax.fori_loop(
        1, lax.axis_size(axis), lambda source, state: combine(state, take(source)), take(0)
    )


def dequantize(table, factor):
    return (table.astype(jnp.float32) * factor).astype(jnp.bfloat16)


def contract_last(left, right):
    return lax.dot_general(
        left, right, (((1,), (1,)), ((), ())), preferred_element_type=jnp.float32
    )


def contract_first(left, right):
    return lax.dot_general(
        left, right, (((0,), (0,)), ((), ())), preferred_element_type=jnp.float32
    )


def merge_two(first, second):
    max_a, sum_a = first
    max_b, sum_b = second
    top = jnp.maximum(max_a, max_b)
    return (top, sum_a * jnp.exp(max_a - top) + sum_b * jnp.exp(max_b - top))


def shards(queries, key_codes, value_codes, key_scale, value_scale, out_grad):
    width = queries.shape[1]
    factor = 1.0 / math.sqrt(width)
    q_full, d_full = (
        lax.all_gather(queries, "ka", axis=0, tiled=True),
        lax.all_gather(out_grad, "ka", axis=0, tiled=True),
    )
    key_rows, value_rows = (
        lax.all_gather(key_codes.astype(jnp.bfloat16), "pb", axis=0, tiled=True),
        lax.all_gather(value_codes.astype(jnp.bfloat16), "pb", axis=0, tiled=True),
    )
    keys = dequantize(key_rows, key_scale)
    values = dequantize(value_rows, value_scale)
    rows = q_full.shape[0]
    block_rows = 512
    block_count = rows // block_rows
    q_blocks = q_full.reshape(block_count, block_rows, width)
    d_blocks = d_full.reshape(block_count, block_rows, width)

    def first_pass(totals, inputs):
        q_block, d_block = inputs
        scores = contract_last(q_block, keys) * factor
        row_max = jnp.max(scores, axis=1)
        shifted = jnp.exp(scores - row_max[:, None])
        d_probs = contract_last(d_block, values)
        return (
            totals,
            (
                row_max,
                jnp.sum(shifted, axis=1),
                jnp.sum(shifted * d_probs, axis=1),
                scores,
                d_probs,
            ),
        )

    _, (row_max, row_sum, row_dot, score_tiles, dprob_tiles) = lax.scan(
        first_pass, jnp.float32(0.0), (q_blocks, d_blocks)
    )
    row_max = row_max.reshape(rows)
    row_sum = row_sum.reshape(rows)
    row_dot = row_dot.reshape(rows)
    full_max, full_sum = merged((row_max, row_sum), "ka", merge_two)
    log_total = full_max + jnp.log(full_sum)
    delta_rows = lax.psum(row_dot * jnp.exp(row_max - log_total), "ka")
    lse_blocks = log_total.reshape(block_count, block_rows)
    delta_blocks = delta_rows.reshape(block_count, block_rows)

    def tile_terms(scores, d_probs, lse_block, delta_block):
        probs = jnp.exp(scores - lse_block[:, None])
        d_scores = probs * (d_probs - delta_block[:, None])
        return (probs.astype(jnp.bfloat16), d_scores.astype(jnp.bfloat16))

    def second_full(totals, inputs):
        k_grad, v_grad = totals
        q_block, d_block, scores, d_probs, lse_block, delta_block = inputs
        probs_low, d_scores_low = tile_terms(scores, d_probs, lse_block, delta_block)
        q_grad = jnp.dot(d_scores_low, keys, preferred_element_type=jnp.float32) * factor
        k_grad = k_grad + contract_first(d_scores_low, q_block) * factor
        v_grad = v_grad + contract_first(probs_low, d_block)
        return ((k_grad, v_grad), q_grad)

    inputs = (q_blocks, d_blocks, score_tiles, dprob_tiles, lse_blocks, delta_blocks)
    zeros = jnp.zeros((keys.shape[0], width), jnp.float32)
    (k_grad, v_grad), q_grad = lax.scan(second_full, (zeros, zeros), inputs)
    stacked = jnp.concatenate([k_grad, v_grad], axis=1)
    summed = lax.psum_scatter(
        stacked.astype(jnp.bfloat16), "pb", scatter_dimension=0, tiled=True
    ).astype(jnp.float32)
    key_grad = summed[:, :width]
    value_grad = summed[:, width:]
    query_grad = lax.psum_scatter(
        q_grad.reshape(rows, width).astype(jnp.bfloat16), "ka", scatter_dimension=0, tiled=True
    ).astype(jnp.float32)
    return (query_grad, key_grad, value_grad)


def solution(mesh):
    in_specs = (
        P(("pb", "ka"), "ha"),
        P(("ka", "pb"), "ha"),
        P(("ka", "pb"), "ha"),
        P(),
        P(),
        P(("pb", "ka"), "ha"),
    )
    out_specs = (P(("pb", "ka"), "ha"), P(("ka", "pb"), "ha"), P(("ka", "pb"), "ha"))
    return jax.shard_map(shards, mesh=mesh, in_specs=in_specs, out_specs=out_specs, check_vma=False)
```

profile of v0, /device:TPU:0, one launch (start us, length us, event | category | flops | bytes accessed | tf_op | source)
XLA Modules:
  0.0 266.3 jit_solution(2322853706921836254)
XLA Ops:
  7.2 0.0 all-gather.5.cloned.1.call-start
  7.2 1.6 convert_element_type.45
  8.8 0.0 all-gather.5.cloned.1.call-update
  8.9 0.0 all-gather.7.cloned.1.call-start
  8.9 1.6 convert_element_type.48
  10.5 0.0 all-gather.7.cloned.1.call-update
  10.6 0.0 reduce-scatter.3.cloned.1.call-start
  12.0 7.4 %all_gather.18 = bf16[1024,128]{1,0:T(8,128)(2,1)S(1)} all-gather(bf16[512,128]{1,0:T(8,128)(2,1)} %param.10), channel_id=1, replica_groups=mesh['pb'=8,'ka'=2,'ha'=2] {'ka'}, dimensions={0}, use_global_device_ids=true | all-gather | bytes 393216 | tf_op jit(solution)/shard_map/all_gather | solution.py:46
  19.3 7.2 %all_gather.20 = bf16[1024,128]{1,0:T(8,128)(2,1)} all-gather(bf16[512,128]{1,0:T(8,128)(2,1)} %param.15), channel_id=1, replica_groups=mesh['pb'=8,'ka'=2,'ha'=2] {'ka'}, dimensions={0}, use_global_device_ids=true | all-gather | bytes 393216 | tf_op jit(solution)/shard_map/all_gather | solution.py:47
  26.5 27.2 %all-gather.5.cloned.1.call-done = bf16[4096,128]{1,0:T(8,128)(2,1)} async-done(((bf16[512,128]{1,0:T(8,128)(2,1)}), bf16[4096,128]{1,0:T(8,128)(2,1)}) %all-gather.5.cloned.1.call-update) | async-done | bytes 1048592 | tf_op jit(solution)/shard_map/all_gather | solution.py:50
  53.6 1.4 multiply_convert_fusion.2
  55.1 40.2 %all-gather.7.cloned.1.call-done = bf16[4096,128]{1,0:T(8,128)(2,1)} async-done(((bf16[512,128]{1,0:T(8,128)(2,1)}), bf16[4096,128]{1,0:T(8,128)(2,1)}) %all-gather.7.cloned.1.call-update) | async-done | bytes 1048592 | tf_op jit(solution)/shard_map/all_gather | solution.py:51
  95.3 2.4 multiply_convert_fusion.1
  97.7 21.8 %while.13 = (s32[]{:T(128)}, f32[2,512]{1,0:T(2,128)S(1)}, f32[2,512]{1,0:T(2,128)S(1)}, f32[2,512]{1,0:T(2,128)S(1)}, f32[2,512,4096]{2,1,0:T(8,128)}, /*index=...) while((s32[]{:T(128)}, f32[2,512]{1,0:T(2,128)S(1)}, ...), condition=%wide.region_4.5_spmd, body=%wide.region_0.4_spmd.sunk | while | flops 1090517504 | bytes 66343616 | solution.py:78
  97.7 0.0 copy-start.1
  97.7 0.0 copy-start.2
  97.7 1.3 multiply_reduce_fusion.4
  99.0 0.0 copy-done.1
  99.0 0.0 copy-done.2
  99.0 3.0 %multiply_reduce_fusion.5 = (f32[512]{0:T(512)S(1)}, f32[512]{0:T(512)S(1)}, f32[512,4096]{1,0:T(8,128)S(1)}) fusion(f32[512,4096]{1,0:T(8,128)S(1)} %get-tuple-element.372, f32[512]{0:T(512)S(1)} %get-tuple-element.371, bf16[4096,128]{1,0:T(8,128)(2,1)S(1)} %copy-done.1, bf16[2,512,128]{2,1,0:T(8,128)(2,1)S(1)} %copy-done.2, s32[]{:T(128)} %get-tuple-element.403), kind=kOutput, calls=%fused_computation.2.clone.1 | convolution fusion | flops 547355648 | bytes 17963012 | tf_op jit(solution)/shard_map/while/body/eval_jaxpr/dot_general | solution.py:24
  102.0 6.4 %bitcast_dynamic-update-slice_fusion.3 = (f32[2,512,4096]{2,1,0:T(8,128)}, f32[2,512,4096]{2,1,0:T(8,128)}) fusion(f32[2,512,4096]{2,1,0:T(8,128)} %get-tuple-element.408, s32[]{:T(128)} %get-tuple-element.403, f32[512,4096]{1,0:T(8,128)S(1)} %get-tuple-element.375, f32[2,512,4096]{2,1,0:T(8,128)} %get-tuple-element.407, ...), kind=kLoop, calls=%fused_computation.clone.1 | loop fusion | flops 2097152 | bytes 33554944 | tf_op jit(solution)/shard_map/while/body/jit(dynamic_update_index_in_dim)/dynamic_update_slice | solution.py:78
  108.6 0.0 copy-start.1
  108.6 0.0 copy-start.2
  108.6 1.3 multiply_reduce_fusion.4
  109.9 0.0 copy-done.1
  109.9 0.0 copy-done.2
  109.9 3.0 %multiply_reduce_fusion.5 = (f32[512]{0:T(512)S(1)}, f32[512]{0:T(512)S(1)}, f32[512,4096]{1,0:T(8,128)S(1)}) fusion(f32[512,4096]{1,0:T(8,128)S(1)} %get-tuple-element.372, f32[512]{0:T(512)S(1)} %get-tuple-element.371, bf16[4096,128]{1,0:T(8,128)(2,1)S(1)} %copy-done.1, bf16[2,512,128]{2,1,0:T(8,128)(2,1)S(1)} %copy-done.2, s32[]{:T(128)} %get-tuple-element.403), kind=kOutput, calls=%fused_computation.2.clone.1 | convolution fusion | flops 547355648 | bytes 17963012 | tf_op jit(solution)/shard_map/while/body/eval_jaxpr/dot_general | solution.py:24
  112.9 6.4 %bitcast_dynamic-update-slice_fusion.3 = (f32[2,512,4096]{2,1,0:T(8,128)}, f32[2,512,4096]{2,1,0:T(8,128)}) fusion(f32[2,512,4096]{2,1,0:T(8,128)} %get-tuple-element.408, s32[]{:T(128)} %get-tuple-element.403, f32[512,4096]{1,0:T(8,128)S(1)} %get-tuple-element.375, f32[2,512,4096]{2,1,0:T(8,128)} %get-tuple-element.407, ...), kind=kLoop, calls=%fused_computation.clone.1 | loop fusion | flops 2097152 | bytes 33554944 | tf_op jit(solution)/shard_map/while/body/jit(dynamic_update_index_in_dim)/dynamic_update_slice | solution.py:78
  119.5 4.3 %all-gather = f32[2,1,1024]{2,1,0:T(1,128)S(1)} all-gather(f32[1,1,1024]{2,1,0:T(1,128)S(1)} %reshape.58), channel_id=1, replica_groups=mesh['pb'=8,'ka'=2,'ha'=2] {'ka'}, dimensions={0}, use_global_device_ids=true | all-gather | bytes 12288 | tf_op jit(solution)/shard_map/all_gather | solution.py:9
  123.8 4.3 %all-gather.1 = f32[2,1,1024]{2,1,0:T(1,128)S(1)} all-gather(f32[1,1,1024]{2,1,0:T(1,128)S(1)} %reshape.60), channel_id=1, replica_groups=mesh['pb'=8,'ka'=2,'ha'=2] {'ka'}, dimensions={0}, use_global_device_ids=true | all-gather | bytes 12288 | tf_op jit(solution)/shard_map/all_gather | solution.py:9
  128.2 4.9 %psum.7 = f32[2,512]{1,0:T(2,128)S(1)} all-reduce(f32[2,512]{1,0:T(2,128)S(1)} %reshape.57), channel_id=1, replica_groups=mesh['pb'=8,'ka'=2,'ha'=2] {'ka'}, use_global_device_ids=true, to_apply=%region_5.6 | all-reduce | flops 1024 | bytes 8192 | tf_op jit(solution)/shard_map/psum | solution.py:86
  133.3 42.3 %while.40 = (s32[]{:T(128)}, f32[4096,128]{1,0:T(8,128)S(1)}, f32[4096,128]{1,0:T(8,128)}, bf16[2,512,128]{2,1,0:T(8,128)(2,1)}, f32[2,512,4096]{2,1,0:T(8,128)}...) while((s32[]{:T(128)}, f32[4096,128]{1,0:T(8,128)S(1)}, ...), condition=%wide.region_7.8_spmd.clone, body=%wide.region_6.7_spmd.clone.sunk | while | flops 1634271232 | bytes 122180872 | solution.py:106
  133.3 0.0 copy-start
  133.3 0.0 copy-start.4
  133.3 9.4 %fusion.65 = f32[4096,128]{1,0:T(8,128)S(1)} fusion(f32[2,512,4096]{2,1,0:T(8,128)} %get-tuple-element.459, s32[]{:T(128)} %get-tuple-element.440, f32[2,512,4096]{2,1,0:T(8,128)} %get-tuple-element.457, f32[512]{0:T(512)S(1)} %bitcast.117, f32[512]{0:T(512)S(1)} %bitcast.114, f32[4096,128]{1,0:T(8,128)S(1)} %get-tuple-element.441, ...), kind=kOutput, calls=%fused_computation.24.clone.1 | convolution fusion | flops 546832384 | bytes 21107712 | tf_op jit(solution)/shard_map/while/body/eval_jaxpr/dot_general | solution.py:30
  142.7 1.2 copy-done
  143.8 0.0 copy-done.4
  143.8 0.0 copy-start.3
  143.8 5.5 %fusion.66 = bf16[2,512,128]{2,1,0:T(8,128)(2,1)S(1)} fusion(bf16[2,512,128]{2,1,0:T(8,128)(2,1)S(1)} %copy-done.4, s32[]{:T(128)} %get-tuple-element.440, bf16[4096,128]{1,0:T(8,128)(2,1)S(1)} %get-tuple-element.463, f32[2,512,4096]{2,1,0:T(8,128)} %get-tuple-element.459, f32[2,512,4096]{2,1,0:T(8,128)S(1)} %copy-done, f32[512]{0:T(512)S(1)} %bitcast.118, ...), kind=kOutput, calls=%fused_computation.33.clone.1 | convolution fusion | flops 545325056 | bytes 18093056 | tf_op jit(solution)/shard_map/while/body/eval_jaxpr/dot_general | solution.py:99
  149.3 0.0 copy-start.5
  149.3 0.7 copy-done.5
  150.0 0.0 copy-done.3
  150.0 3.6 %convolution_add_fusion.2 = f32[4096,128]{1,0:T(8,128)} fusion(f32[2,512,4096]{2,1,0:T(8,128)S(1)} %copy-done, s32[]{:T(128)} %get-tuple-element.440, f32[512]{0:T(512)S(1)} %bitcast.116, f32[4096,128]{1,0:T(8,128)} %get-tuple-element.442, pred[]{:T(512)S(6)} %compare.3, bf16[2,512,128]{2,1,0:T(8,128)(2,1)S(1)} %copy-done.3), kind=kOutput, calls=%fused_computation.22.clone.1 | convolution fusion | flops 542113792 | bytes 12717057 | tf_op jit(solution)/shard_map/while/body/eval_jaxpr/dot_general | solution.py:30
  153.6 0.0 copy-start
  153.7 0.0 copy-start.4
  153.7 9.4 %fusion.65 = f32[4096,128]{1,0:T(8,128)S(1)} fusion(f32[2,512,4096]{2,1,0:T(8,128)} %get-tuple-element.459, s32[]{:T(128)} %get-tuple-element.440, f32[2,512,4096]{2,1,0:T(8,128)} %get-tuple-element.457, f32[512]{0:T(512)S(1)} %bitcast.117, f32[512]{0:T(512)S(1)} %bitcast.114, f32[4096,128]{1,0:T(8,128)S(1)} %get-tuple-element.441, ...), kind=kOutput, calls=%fused_computation.24.clone.1 | convolution fusion | flops 546832384 | bytes 21107712 | tf_op jit(solution)/shard_map/while/body/eval_jaxpr/dot_general | solution.py:30
  163.0 1.2 copy-done
  164.2 0.0 copy-done.4
  164.2 0.0 copy-start.3
  164.2 5.5 %fusion.66 = bf16[2,512,128]{2,1,0:T(8,128)(2,1)S(1)} fusion(bf16[2,512,128]{2,1,0:T(8,128)(2,1)S(1)} %copy-done.4, s32[]{:T(128)} %get-tuple-element.440, bf16[4096,128]{1,0:T(8,128)(2,1)S(1)} %get-tuple-element.463, f32[2,512,4096]{2,1,0:T(8,128)} %get-tuple-element.459, f32[2,512,4096]{2,1,0:T(8,128)S(1)} %copy-done, f32[512]{0:T(512)S(1)} %bitcast.118, ...), kind=kOutput, calls=%fused_computation.33.clone.1 | convolution fusion | flops 545325056 | bytes 18093056 | tf_op jit(solution)/shard_map/while/body/eval_jaxpr/dot_general | solution.py:99
  169.7 0.0 copy-start.5
  169.7 0.7 copy-done.5
  170.4 0.0 copy-done.3
  170.4 5.2 %convolution_add_fusion.2 = f32[4096,128]{1,0:T(8,128)} fusion(f32[2,512,4096]{2,1,0:T(8,128)S(1)} %copy-done, s32[]{:T(128)} %get-tuple-element.440, f32[512]{0:T(512)S(1)} %bitcast.116, f32[4096,128]{1,0:T(8,128)} %get-tuple-element.442, pred[]{:T(512)S(6)} %compare.3, bf16[2,512,128]{2,1,0:T(8,128)(2,1)S(1)} %copy-done.3), kind=kOutput, calls=%fused_computation.22.clone.1 | convolution fusion | flops 542113792 | bytes 12717057 | tf_op jit(solution)/shard_map/while/body/eval_jaxpr/dot_general | solution.py:30
  175.6 0.0 reduce-scatter.3.cloned.1.call-update
  175.6 0.0 reduce-scatter.5.cloned.1.call-start
  175.6 0.1 convert.6
  175.8 1.7 convert.7
  177.5 1.6 pad_maximum_fusion
  179.0 0.0 reduce-scatter.5.cloned.1.call-update
  179.1 7.1 %reduce-scatter.3.cloned.1.call-done = bf16[512,128]{1,0:T(8,128)(2,1)} async-done(((bf16[1024,128]{1,0:T(8,128)(2,1)}), bf16[512,128]{1,0:T(8,128)(2,1)}) %reduce-scatter.3.cloned.1.call-update) | async-done | bytes 131088 | tf_op jit(solution)/shard_map/reduce_scatter | solution.py:113
  186.2 1.6 convert_element_type.53
  187.8 70.2 %reduce-scatter.5.cloned.1.call-done = bf16[512,256]{1,0:T(8,128)(2,1)} async-done(((bf16[4096,256]{1,0:T(8,128)(2,1)}), bf16[512,256]{1,0:T(8,128)(2,1)}) %reduce-scatter.5.cloned.1.call-update) | async-done | bytes 262160 | tf_op jit(solution)/shard_map/reduce_scatter | solution.py:108
  258.0 1.8 fusion.43
  (28 shorter events, 0.4 us)
Async XLA Ops:
  7.2 46.5 %all-gather.5.cloned.1.call-start = ((), (), s32[]{:S(2)}) async-start(), calls=%async_computation.2 | async-start | bytes 1179648 | tf_op jit(solution)/shard_map/all_gather | solution.py:50
  8.9 86.4 %all-gather.7.cloned.1.call-start = ((), (), s32[]{:S(2)}) async-start(), calls=%async_computation.3 | async-start | bytes 1179648 | tf_op jit(solution)/shard_map/all_gather | solution.py:51
  10.6 175.6 %reduce-scatter.3.cloned.1.call-start = ((), (), s32[]{:S(2)}) async-start(), calls=%async_computation.4 | async-start | bytes 393216 | tf_op jit(solution)/shard_map/reduce_scatter | solution.py:113
  97.7 1.3 copy-start.1
  97.7 1.3 copy-start.2
  108.6 1.4 copy-start.1
  108.6 1.4 copy-start.2
  133.3 10.5 %copy-start = (f32[2,512,4096]{2,1,0:T(8,128)S(1)}, f32[2,512,4096]{2,1,0:T(8,128)}, u32[]{:S(2)}) copy-start(f32[2,512,4096]{2,1,0:T(8,128)} %get-tuple-element.457) | copy-start | bytes 50331652 | tf_op jit(solution)/shard_map/while
  133.3 10.5 %copy-start.4 = (bf16[2,512,128]{2,1,0:T(8,128)(2,1)S(1)}, bf16[2,512,128]{2,1,0:T(8,128)(2,1)}, u32[]{:S(2)}) copy-start(bf16[2,512,128]{2,1,0:T(8,128)(2,1)} %get-tuple-element.443) | copy-start | bytes 786436 | tf_op jit(solution)/shard_map/while
  143.8 6.2 %copy-start.3 = (bf16[2,512,128]{2,1,0:T(8,128)(2,1)S(1)}, bf16[2,512,128]{2,1,0:T(8,128)(2,1)}, u32[]{:S(2)}) copy-start(bf16[2,512,128]{2,1,0:T(8,128)(2,1)} %get-tuple-element.462) | copy-start | bytes 786436 | tf_op jit(solution)/shard_map/while
  149.3 0.7 copy-start.5
  153.6 10.5 %copy-start = (f32[2,512,4096]{2,1,0:T(8,128)S(1)}, f32[2,512,4096]{2,1,0:T(8,128)}, u32[]{:S(2)}) copy-start(f32[2,512,4096]{2,1,0:T(8,128)} %get-tuple-element.457) | copy-start | bytes 50331652 | tf_op jit(solution)/shard_map/while
  153.7 10.5 %copy-start.4 = (bf16[2,512,128]{2,1,0:T(8,128)(2,1)S(1)}, bf16[2,512,128]{2,1,0:T(8,128)(2,1)}, u32[]{:S(2)}) copy-start(bf16[2,512,128]{2,1,0:T(8,128)(2,1)} %get-tuple-element.443) | copy-start | bytes 786436 | tf_op jit(solution)/shard_map/while
  164.2 6.2 %copy-start.3 = (bf16[2,512,128]{2,1,0:T(8,128)(2,1)S(1)}, bf16[2,512,128]{2,1,0:T(8,128)(2,1)}, u32[]{:S(2)}) copy-start(bf16[2,512,128]{2,1,0:T(8,128)(2,1)} %get-tuple-element.462) | copy-start | bytes 786436 | tf_op jit(solution)/shard_map/while
  169.7 0.7 copy-start.5
  175.6 82.4 %reduce-scatter.5.cloned.1.call-start = ((), (), s32[]{:S(2)}) async-start(), calls=%async_computation.5 | async-start | bytes 2359296 | tf_op jit(solution)/shard_map/reduce_scatter | solution.py:108
Sparse Core Ops, SparseCore 0:
  10.7 42.9 all-gather.4
  56.3 38.8 all-gather.6
  175.7 10.4 reduce-scatter.2
  190.0 67.9 reduce-scatter.4
where the time goes:
time: 267 us; the launch traced here: 266 us
  waiting for transfers between devices  145 us (54%)
  matrix products  47.1 us (18%)
  blocking collectives  28.1 us (11%)
  other arithmetic  24.9 us (9%)
  between operations  15.2 us (6%)
  local copies, waits for them, and re-layouts  5.91 us (2%)
    reduce_scatter x1, waiting for transfers between devices, shards(): lax.psum_scatter(stacked.astype(jnp.bfloat16), 'pb', scatter_dimension=0,...  70.2 us
    all_gather x1, waiting for transfers between devices, shards(): lax.all_gather(value_codes.astype(jnp.bfloat16), 'pb', axis=0, tiled=True)  40.2 us
    dot_general x4, matrix products, contract_first(): lax.dot_general(left, right, (((0,), (0,)), ((), ())), preferred_element_...  27.5 us
    all_gather x1, waiting for transfers between devices, shards(): lax.all_gather(key_codes.astype(jnp.bfloat16), 'pb', axis=0, tiled=True)  27.2 us
    dynamic_update_slice x2, other arithmetic, shards(): lax.scan(first_pass, jnp.float32(0.0), (q_blocks, d_blocks))  12.8 us
    dot_general x2, matrix products, second_full(): jnp.dot(d_scores_low, keys, preferred_element_type=jnp.float32) * factor  11 us
    all_gather x2, blocking collectives, merged(): gathered = jax.tree.map(lambda a: lax.all_gather(a, axis), part)  8.68 us
    dot_general x4, matrix products, contract_last(): lax.dot_general(left, right, (((1,), (1,)), ((), ())), preferred_element_...  8.63 us
  transfers between devices with their start and end apart: 4, of which 4 were waited for; matrix products, arithmetic and copies ran while one was open for 3% of the time, Pallas kernels for 0%

commit v1 on v0

--- a/solution.py
+++ b/solution.py
@@ -3,6 +3,19 @@
 import jax.numpy as jnp
 from jax import lax
 from jax.sharding import PartitionSpec as P
+
+
+def collect(value, axis, dim):
+    ways = lax.axis_size(axis)
+    up = [(d, (d + 1) % ways) for d in range(ways)]
+    down = [(d, (d - 1) % ways) for d in range(ways)]
+    earlier, later = ([value], [value])
+    for _ in range(ways // 2):
+        earlier.append(lax.ppermute(earlier[-1], axis, up))
+    for _ in range((ways - 1) // 2):
+        later.append(lax.ppermute(later[-1], axis, down))
+    line = jnp.concatenate([*earlier[::-1], *later[1:]], axis=dim)
+    return jnp.roll(line, (lax.axis_index(axis) - ways // 2) * value.shape[dim], axis=dim)
 
 
 def merged(part, axis, combine):
@@ -48,7 +61,7 @@
     )
     key_rows, value_rows = (
         lax.all_gather(key_codes.astype(jnp.bfloat16), "pb", axis=0, tiled=True),
-        lax.all_gather(value_codes.astype(jnp.bfloat16), "pb", axis=0, tiled=True),
+        collect(value_codes.astype(jnp.bfloat16), "pb", 0),
     )
     keys = dequantize(key_rows, key_scale)
     values = dequantize(value_rows, value_scale)

time: 267 us -> 240 us (0.90)
  waiting for transfers between devices: 145 us -> 104 us
  starting transfers between devices: 0.16 us -> 17.4 us
    all_gather x1 -> x0, waiting for transfers between devices: 40.2 us -> none  [shards(): lax.all_gather(value_codes.astype(jnp.bfloat16), 'pb', axis=0, tiled=True)]
    ppermute x0 -> x7, starting transfers between devices: none -> 17.2 us  [the longest x3 14.2 us: collect(): later.append(lax.ppermute(later[-1], axis, down))]
    all_gather x1, waiting for transfers between devices: 27.2 us -> 14.5 us  [shards(): lax.all_gather(key_codes.astype(jnp.bfloat16), 'pb', axis=0, tiled=True)]
    ppermute x0 -> x7, waiting for transfers between devices: none -> 11.9 us  [the longest x4 9.54 us: collect(): earlier.append(lax.ppermute(earlier[-1], axis, up))]
  transfers between devices with their start and end apart: 4 -> 10, of which waited for: 4 -> 6; matrix products, arithmetic and copies ran while one was open for 3% -> 3% of each run, Pallas kernels for 0% -> 0%
where the time goes in v1:
time: 240 us; the launch traced here: 239 us
  waiting for transfers between devices  104 us (43%)
  matrix products  47.1 us (20%)
  blocking collectives  26.4 us (11%)
  other arithmetic  23.1 us (10%)
  starting transfers between devices  17.4 us (7%)
  between operations  15.3 us (6%)
  local copies, waits for them, and re-layouts  6.18 us (3%)
    reduce_scatter x1, waiting for transfers between devices, shards(): lax.psum_scatter(stacked.astype(jnp.bfloat16), 'pb', scatter_dimension=0,...  70 us
    dot_general x4, matrix products, contract_first(): lax.dot_general(left, right, (((0,), (0,)), ((), ())), preferred_element_...  27.5 us
    all_gather x1, waiting for transfers between devices, shards(): lax.all_gather(key_codes.astype(jnp.bfloat16), 'pb', axis=0, tiled=True)  14.5 us
    ppermute x3, starting transfers between devices, collect(): later.append(lax.ppermute(later[-1], axis, down))  14.2 us
    dynamic_update_slice x2, other arithmetic, shards(): lax.scan(first_pass, jnp.float32(0.0), (q_blocks, d_blocks))  12.8 us
    dot_general x2, matrix products, second_full(): jnp.dot(d_scores_low, keys, preferred_element_type=jnp.float32) * factor  11 us
    ppermute x4, waiting for transfers between devices, collect(): earlier.append(lax.ppermute(earlier[-1], axis, up))  9.54 us
    all_gather x2, blocking collectives, merged(): gathered = jax.tree.map(lambda a: lax.all_gather(a, axis), part)  8.68 us
  transfers between devices with their start and end apart: 10, of which 6 were waited for; matrix products, arithmetic and copies ran while one was open for 3% of the time, Pallas kernels for 0%

profile of v1, /device:TPU:0, one launch (start us, length us, event | category | flops | bytes accessed | tf_op | source)
XLA Modules:
  0.0 239.3 jit_solution(15791258078670510426)
XLA Ops:
  7.2 0.0 copy-start.4
  7.2 0.0 all-gather.4.cloned.1.call-start
  7.2 1.0 convert_element_type.48
  8.2 3.0 %collective-permute-start = (bf16[512,128]{1,0:T(8,128)(2,1)S(1)}, bf16[512,128]{1,0:T(8,128)(2,1)S(1)}, u32[]{:S(2)}, u32[]{:S(2)}) collective-permute-start(bf16[512,128]{1,0:T(8,128)(2,1)S(1)} %convert_element_type.48), channel_id=1, source_target_pairs={{0,4},{4,8},{8,12},{12,16},{16,20},{20,24},{24,28},{28,0},{1,5},{5... | collective-permute-start | bytes 393224 | tf_op jit(solution)/shard_map/ppermute | solution.py:14
  11.2 6.5 %collective-permute-done = bf16[512,128]{1,0:T(8,128)(2,1)S(1)} collective-permute-done((bf16[512,128]{1,0:T(8,128)(2,1)S(1)}, bf16[512,128]{1,0:T(8,128)(2,1)S(1)}, u32[]{:S(2)}, u32[]{:S(2)}) %collective-permute-start) | collective-permute-done | bytes 131104 | tf_op jit(solution)/shard_map/ppermute | solution.py:14
  17.8 0.0 collective-permute-start.1
  17.8 4.7 %collective-permute-start.4 = (bf16[512,128]{1,0:T(8,128)(2,1)S(1)}, bf16[512,128]{1,0:T(8,128)(2,1)S(1)}, u32[]{:S(2)}, u32[]{:S(2)}) collective-permute-start(bf16[512,128]{1,0:T(8,128)(2,1)S(1)} %convert_element_type.48), channel_id=1, source_target_pairs={{0,28},{4,0},{8,4},{12,8},{16,12},{20,16},{24,20},{28,24},{1,29},{... | collective-permute-start | bytes 393224 | tf_op jit(solution)/shard_map/ppermute | solution.py:16
  22.5 3.0 %collective-permute-done.1 = bf16[512,128]{1,0:T(8,128)(2,1)S(1)} collective-permute-done((bf16[512,128]{1,0:T(8,128)(2,1)S(1)}, bf16[512,128]{1,0:T(8,128)(2,1)S(1)}, u32[]{:S(2)}, u32[]{:S(2)}) %collective-permute-start.1) | collective-permute-done | bytes 131104 | tf_op jit(solution)/shard_map/ppermute | solution.py:14
  25.5 0.1 collective-permute-start.2
  25.6 1.6 convert_element_type.45
  27.2 0.0 all-gather.4.cloned.1.call-update
  27.2 0.0 reduce-scatter.3.cloned.1.call-start
  28.7 0.0 collective-permute-done.4
  28.7 4.7 %collective-permute-start.5 = (bf16[512,128]{1,0:T(8,128)(2,1)S(1)}, bf16[512,128]{1,0:T(8,128)(2,1)S(1)}, u32[]{:S(2)}, u32[]{:S(2)}) collective-permute-start(bf16[512,128]{1,0:T(8,128)(2,1)S(1)} %collective-permute-done.4), channel_id=1, source_target_pairs={{0,28},{4,0},{8,4},{12,8},{16,12},{20,16},{24,20},{28,24},{1,29},{... | collective-permute-start | bytes 393224 | tf_op jit(solution)/shard_map/ppermute | solution.py:16
  33.4 0.0 collective-permute-done.2
  33.4 0.0 collective-permute-start.3
  33.4 5.8 %all_gather.15 = bf16[1024,128]{1,0:T(8,128)(2,1)S(1)} all-gather(bf16[512,128]{1,0:T(8,128)(2,1)} %param.10), channel_id=1, replica_groups=mesh['pb'=8,'ka'=2,'ha'=2] {'ka'}, dimensions={0}, use_global_device_ids=true | all-gather | bytes 393216 | tf_op jit(solution)/shard_map/all_gather | solution.py:59
  39.2 7.0 %all_gather.17 = bf16[1024,128]{1,0:T(8,128)(2,1)} all-gather(bf16[512,128]{1,0:T(8,128)(2,1)} %param.15), channel_id=1, replica_groups=mesh['pb'=8,'ka'=2,'ha'=2] {'ka'}, dimensions={0}, use_global_device_ids=true | all-gather | bytes 393216 | tf_op jit(solution)/shard_map/all_gather | solution.py:60
  46.2 0.0 collective-permute-done.5
  46.2 4.7 %collective-permute-start.6 = (bf16[512,128]{1,0:T(8,128)(2,1)S(1)}, bf16[512,128]{1,0:T(8,128)(2,1)S(1)}, u32[]{:S(2)}, u32[]{:S(2)}) collective-permute-start(bf16[512,128]{1,0:T(8,128)(2,1)S(1)} %collective-permute-done.5), channel_id=1, source_target_pairs={{0,28},{4,0},{8,4},{12,8},{16,12},{20,16},{24,20},{28,24},{1,29},{... | collective-permute-start | bytes 393224 | tf_op jit(solution)/shard_map/ppermute | solution.py:16
  50.9 0.0 collective-permute-done.3
  51.0 0.0 copy-done.4
  51.1 2.3 collective-permute-done.6
  53.7 1.2 multiply_convert_fusion.1
  54.9 14.5 %all-gather.4.cloned.1.call-done = bf16[4096,128]{1,0:T(8,128)(2,1)} async-done(((bf16[512,128]{1,0:T(8,128)(2,1)}), bf16[4096,128]{1,0:T(8,128)(2,1)}) %all-gather.4.cloned.1.call-update) | async-done | bytes 1048592 | tf_op jit(solution)/shard_map/all_gather | solution.py:63
  69.4 1.4 multiply_convert_fusion.2
  70.8 21.8 %while.13 = (s32[]{:T(128)}, f32[2,512]{1,0:T(2,128)S(1)}, f32[2,512]{1,0:T(2,128)S(1)}, f32[2,512]{1,0:T(2,128)S(1)}, f32[2,512,4096]{2,1,0:T(8,128)}, /*index=...) while((s32[]{:T(128)}, f32[2,512]{1,0:T(2,128)S(1)}, ...), condition=%wide.region_4.5_spmd, body=%wide.region_0.4_spmd.sunk | while | flops 1090517504 | bytes 66343616 | solution.py:91
  70.8 1.3 multiply_reduce_fusion.4
  72.2 3.0 %multiply_reduce_fusion.5 = (f32[512]{0:T(512)S(1)}, f32[512]{0:T(512)S(1)}, f32[512,4096]{1,0:T(8,128)S(1)}) fusion(f32[512,4096]{1,0:T(8,128)S(1)} %get-tuple-element.372, f32[512]{0:T(512)S(1)} %get-tuple-element.371, bf16[4096,128]{1,0:T(8,128)(2,1)S(1)} %copy-done.1, bf16[2,512,128]{2,1,0:T(8,128)(2,1)S(1)} %copy-done.2, s32[]{:T(128)} %get-tuple-element.403), kind=kOutput, calls=%fused_computation.2.clone.1 | convolution fusion | flops 547355648 | bytes 17963012 | tf_op jit(solution)/shard_map/while/body/eval_jaxpr/dot_general | solution.py:37
  75.2 6.4 %bitcast_dynamic-update-slice_fusion.3 = (f32[2,512,4096]{2,1,0:T(8,128)}, f32[2,512,4096]{2,1,0:T(8,128)}) fusion(f32[2,512,4096]{2,1,0:T(8,128)} %get-tuple-element.408, s32[]{:T(128)} %get-tuple-element.403, f32[512,4096]{1,0:T(8,128)S(1)} %get-tuple-element.375, f32[2,512,4096]{2,1,0:T(8,128)} %get-tuple-element.407, ...), kind=kLoop, calls=%fused_computation.clone.1 | loop fusion | flops 2097152 | bytes 33554944 | tf_op jit(solution)/shard_map/while/body/jit(dynamic_update_index_in_dim)/dynamic_update_slice | solution.py:91
  81.7 1.3 multiply_reduce_fusion.4
  83.1 0.0 copy-done.2
  83.1 3.0 %multiply_reduce_fusion.5 = (f32[512]{0:T(512)S(1)}, f32[512]{0:T(512)S(1)}, f32[512,4096]{1,0:T(8,128)S(1)}) fusion(f32[512,4096]{1,0:T(8,128)S(1)} %get-tuple-element.372, f32[512]{0:T(512)S(1)} %get-tuple-element.371, bf16[4096,128]{1,0:T(8,128)(2,1)S(1)} %copy-done.1, bf16[2,512,128]{2,1,0:T(8,128)(2,1)S(1)} %copy-done.2, s32[]{:T(128)} %get-tuple-element.403), kind=kOutput, calls=%fused_computation.2.clone.1 | convolution fusion | flops 547355648 | bytes 17963012 | tf_op jit(solution)/shard_map/while/body/eval_jaxpr/dot_general | solution.py:37
  86.1 6.4 %bitcast_dynamic-update-slice_fusion.3 = (f32[2,512,4096]{2,1,0:T(8,128)}, f32[2,512,4096]{2,1,0:T(8,128)}) fusion(f32[2,512,4096]{2,1,0:T(8,128)} %get-tuple-element.408, s32[]{:T(128)} %get-tuple-element.403, f32[512,4096]{1,0:T(8,128)S(1)} %get-tuple-element.375, f32[2,512,4096]{2,1,0:T(8,128)} %get-tuple-element.407, ...), kind=kLoop, calls=%fused_computation.clone.1 | loop fusion | flops 2097152 | bytes 33554944 | tf_op jit(solution)/shard_map/while/body/jit(dynamic_update_index_in_dim)/dynamic_update_slice | solution.py:91
  92.6 4.3 %all-gather = f32[2,1,1024]{2,1,0:T(1,128)S(1)} all-gather(f32[1,1,1024]{2,1,0:T(1,128)S(1)} %reshape.58), channel_id=1, replica_groups=mesh['pb'=8,'ka'=2,'ha'=2] {'ka'}, dimensions={0}, use_global_device_ids=true | all-gather | bytes 12288 | tf_op jit(solution)/shard_map/all_gather | solution.py:22
  97.0 4.3 %all-gather.1 = f32[2,1,1024]{2,1,0:T(1,128)S(1)} all-gather(f32[1,1,1024]{2,1,0:T(1,128)S(1)} %reshape.60), channel_id=1, replica_groups=mesh['pb'=8,'ka'=2,'ha'=2] {'ka'}, dimensions={0}, use_global_device_ids=true | all-gather | bytes 12288 | tf_op jit(solution)/shard_map/all_gather | solution.py:22
  101.4 4.9 %psum.7 = f32[2,512]{1,0:T(2,128)S(1)} all-reduce(f32[2,512]{1,0:T(2,128)S(1)} %reshape.57), channel_id=1, replica_groups=mesh['pb'=8,'ka'=2,'ha'=2] {'ka'}, use_global_device_ids=true, to_apply=%region_5.6 | all-reduce | flops 1024 | bytes 8192 | tf_op jit(solution)/shard_map/psum | solution.py:99
  106.4 42.3 %while.40 = (s32[]{:T(128)}, f32[4096,128]{1,0:T(8,128)S(1)}, f32[4096,128]{1,0:T(8,128)}, bf16[2,512,128]{2,1,0:T(8,128)(2,1)}, f32[2,512,4096]{2,1,0:T(8,128)}...) while((s32[]{:T(128)}, f32[4096,128]{1,0:T(8,128)S(1)}, ...), condition=%wide.region_7.8_spmd.clone, body=%wide.region_6.7_spmd.clone.sunk | while | flops 1634271232 | bytes 122180872 | solution.py:119
  106.4 0.0 copy-start.5
  106.5 9.4 %fusion.65 = f32[4096,128]{1,0:T(8,128)S(1)} fusion(f32[2,512,4096]{2,1,0:T(8,128)} %get-tuple-element.459, s32[]{:T(128)} %get-tuple-element.440, f32[2,512,4096]{2,1,0:T(8,128)} %get-tuple-element.457, f32[512]{0:T(512)S(1)} %bitcast.117, f32[512]{0:T(512)S(1)} %bitcast.114, f32[4096,128]{1,0:T(8,128)S(1)} %get-tuple-element.441, ...), kind=kOutput, calls=%fused_computation.24.clone.1 | convolution fusion | flops 546832384 | bytes 21107712 | tf_op jit(solution)/shard_map/while/body/eval_jaxpr/dot_general | solution.py:43
  115.8 1.2 copy-done
  117.0 5.5 %fusion.66 = bf16[2,512,128]{2,1,0:T(8,128)(2,1)S(1)} fusion(bf16[2,512,128]{2,1,0:T(8,128)(2,1)S(1)} %copy-done.5, s32[]{:T(128)} %get-tuple-element.440, bf16[4096,128]{1,0:T(8,128)(2,1)S(1)} %get-tuple-element.463, f32[2,512,4096]{2,1,0:T(8,128)} %get-tuple-element.459, f32[2,512,4096]{2,1,0:T(8,128)S(1)} %copy-done, f32[512]{0:T(512)S(1)} %bitcast.118, ...), kind=kOutput, calls=%fused_computation.33.clone.1 | convolution fusion | flops 545325056 | bytes 18093056 | tf_op jit(solution)/shard_map/while/body/eval_jaxpr/dot_general | solution.py:112
  122.5 0.0 copy-start.6
  122.5 0.7 copy-done.6
  123.2 3.6 %convolution_add_fusion.2 = f32[4096,128]{1,0:T(8,128)} fusion(f32[2,512,4096]{2,1,0:T(8,128)S(1)} %copy-done, s32[]{:T(128)} %get-tuple-element.440, f32[512]{0:T(512)S(1)} %bitcast.116, f32[4096,128]{1,0:T(8,128)} %get-tuple-element.442, pred[]{:T(512)S(6)} %compare.4, bf16[2,512,128]{2,1,0:T(8,128)(2,1)S(1)} %copy-done.3), kind=kOutput, calls=%fused_computation.22.clone.1 | convolution fusion | flops 542113792 | bytes 12717057 | tf_op jit(solution)/shard_map/while/body/eval_jaxpr/dot_general | solution.py:43
  126.8 0.0 copy-start.5
  126.8 9.4 %fusion.65 = f32[4096,128]{1,0:T(8,128)S(1)} fusion(f32[2,512,4096]{2,1,0:T(8,128)} %get-tuple-element.459, s32[]{:T(128)} %get-tuple-element.440, f32[2,512,4096]{2,1,0:T(8,128)} %get-tuple-element.457, f32[512]{0:T(512)S(1)} %bitcast.117, f32[512]{0:T(512)S(1)} %bitcast.114, f32[4096,128]{1,0:T(8,128)S(1)} %get-tuple-element.441, ...), kind=kOutput, calls=%fused_computation.24.clone.1 | convolution fusion | flops 546832384 | bytes 21107712 | tf_op jit(solution)/shard_map/while/body/eval_jaxpr/dot_general | solution.py:43
  136.2 1.2 copy-done
  137.3 0.0 copy-done.5
  137.3 5.5 %fusion.66 = bf16[2,512,128]{2,1,0:T(8,128)(2,1)S(1)} fusion(bf16[2,512,128]{2,1,0:T(8,128)(2,1)S(1)} %copy-done.5, s32[]{:T(128)} %get-tuple-element.440, bf16[4096,128]{1,0:T(8,128)(2,1)S(1)} %get-tuple-element.463, f32[2,512,4096]{2,1,0:T(8,128)} %get-tuple-element.459, f32[2,512,4096]{2,1,0:T(8,128)S(1)} %copy-done, f32[512]{0:T(512)S(1)} %bitcast.118, ...), kind=kOutput, calls=%fused_computation.33.clone.1 | convolution fusion | flops 545325056 | bytes 18093056 | tf_op jit(solution)/shard_map/while/body/eval_jaxpr/dot_general | solution.py:112
  142.8 0.0 copy-start.6
  142.8 0.7 copy-done.6
  143.5 0.0 copy-done.3
  143.5 5.2 %convolution_add_fusion.2 = f32[4096,128]{1,0:T(8,128)} fusion(f32[2,512,4096]{2,1,0:T(8,128)S(1)} %copy-done, s32[]{:T(128)} %get-tuple-element.440, f32[512]{0:T(512)S(1)} %bitcast.116, f32[4096,128]{1,0:T(8,128)} %get-tuple-element.442, pred[]{:T(512)S(6)} %compare.4, bf16[2,512,128]{2,1,0:T(8,128)(2,1)S(1)} %copy-done.3), kind=kOutput, calls=%fused_computation.22.clone.1 | convolution fusion | flops 542113792 | bytes 12717057 | tf_op jit(solution)/shard_map/while/body/eval_jaxpr/dot_general | solution.py:43
  148.7 0.0 reduce-scatter.3.cloned.1.call-update
  148.7 0.0 reduce-scatter.5.cloned.1.call-start
  148.8 0.1 convert.6
  148.9 1.7 convert.7
  150.6 1.6 pad_maximum_fusion
  152.2 0.0 reduce-scatter.5.cloned.1.call-update
  152.2 7.1 %reduce-scatter.3.cloned.1.call-done = bf16[512,128]{1,0:T(8,128)(2,1)} async-done(((bf16[1024,128]{1,0:T(8,128)(2,1)}), bf16[512,128]{1,0:T(8,128)(2,1)}) %reduce-scatter.3.cloned.1.call-update) | async-done | bytes 131088 | tf_op jit(solution)/shard_map/reduce_scatter | solution.py:126
  159.3 1.6 convert_element_type.53
  160.9 70.0 %reduce-scatter.5.cloned.1.call-done = bf16[512,256]{1,0:T(8,128)(2,1)} async-done(((bf16[4096,256]{1,0:T(8,128)(2,1)}), bf16[512,256]{1,0:T(8,128)(2,1)}) %reduce-scatter.5.cloned.1.call-update) | async-done | bytes 262160 | tf_op jit(solution)/shard_map/reduce_scatter | solution.py:121
  231.0 1.8 fusion.43
  (57 shorter events, 0.8 us)
Async XLA Ops:
  7.2 43.8 %copy-start.4 = (s32[512,128]{1,0:T(8,128)S(1)}, s32[512,128]{1,0:T(8,128)}, u32[]{:S(2)}) copy-start(s32[512,128]{1,0:T(8,128)} %param.12) | copy-start | bytes 786436
  7.2 62.2 %all-gather.4.cloned.1.call-start = ((), (), s32[]{:S(2)}) async-start(), calls=%async_computation.2 | async-start | bytes 1179648 | tf_op jit(solution)/shard_map/all_gather | solution.py:63
  8.2 9.6 %collective-permute-start = (bf16[512,128]{1,0:T(8,128)(2,1)S(1)}, bf16[512,128]{1,0:T(8,128)(2,1)S(1)}, u32[]{:S(2)}, u32[]{:S(2)}) collective-permute-start(bf16[512,128]{1,0:T(8,128)(2,1)S(1)} %convert_element_type.48), channel_id=1, source_target_pairs={{0,4},{4,8},{8,12},{12,16},{16,20},{20,24},{24,28},{28,0},{1,5},{5... | collective-permute-start | bytes 393224 | tf_op jit(solution)/shard_map/ppermute | solution.py:14
  17.8 7.7 %collective-permute-start.1 = (bf16[512,128]{1,0:T(8,128)(2,1)S(1)}, bf16[512,128]{1,0:T(8,128)(2,1)S(1)}, u32[]{:S(2)}, u32[]{:S(2)}) collective-permute-start(bf16[512,128]{1,0:T(8,128)(2,1)S(1)} %collective-permute-done), channel_id=1, source_target_pairs={{0,4},{4,8},{8,12},{12,16},{16,20},{20,24},{24,28},{28,0},{1,5},{5... | collective-permute-start | bytes 393224 | tf_op jit(solution)/shard_map/ppermute | solution.py:14
  17.8 10.9 %collective-permute-start.4 = (bf16[512,128]{1,0:T(8,128)(2,1)S(1)}, bf16[512,128]{1,0:T(8,128)(2,1)S(1)}, u32[]{:S(2)}, u32[]{:S(2)}) collective-permute-start(bf16[512,128]{1,0:T(8,128)(2,1)S(1)} %convert_element_type.48), channel_id=1, source_target_pairs={{0,28},{4,0},{8,4},{12,8},{16,12},{20,16},{24,20},{28,24},{1,29},{... | collective-permute-start | bytes 393224 | tf_op jit(solution)/shard_map/ppermute | solution.py:16
  25.5 7.9 %collective-permute-start.2 = (bf16[512,128]{1,0:T(8,128)(2,1)S(1)}, bf16[512,128]{1,0:T(8,128)(2,1)S(1)}, u32[]{:S(2)}, u32[]{:S(2)}) collective-permute-start(bf16[512,128]{1,0:T(8,128)(2,1)S(1)} %collective-permute-done.1), channel_id=1, source_target_pairs={{0,4},{4,8},{8,12},{12,16},{16,20},{20,24},{24,28},{28,0},{1,5},{5... | collective-permute-start | bytes 393224 | tf_op jit(solution)/shard_map/ppermute | solution.py:14
  27.2 132.1 %reduce-scatter.3.cloned.1.call-start = ((), (), s32[]{:S(2)}) async-start(), calls=%async_computation.3 | async-start | bytes 393216 | tf_op jit(solution)/shard_map/reduce_scatter | solution.py:126
  28.7 17.5 %collective-permute-start.5 = (bf16[512,128]{1,0:T(8,128)(2,1)S(1)}, bf16[512,128]{1,0:T(8,128)(2,1)S(1)}, u32[]{:S(2)}, u32[]{:S(2)}) collective-permute-start(bf16[512,128]{1,0:T(8,128)(2,1)S(1)} %collective-permute-done.4), channel_id=1, source_target_pairs={{0,28},{4,0},{8,4},{12,8},{16,12},{20,16},{24,20},{28,24},{1,29},{... | collective-permute-start | bytes 393224 | tf_op jit(solution)/shard_map/ppermute | solution.py:16
  33.4 17.5 %collective-permute-start.3 = (bf16[512,128]{1,0:T(8,128)(2,1)S(1)}, bf16[512,128]{1,0:T(8,128)(2,1)S(1)}, u32[]{:S(2)}, u32[]{:S(2)}) collective-permute-start(bf16[512,128]{1,0:T(8,128)(2,1)S(1)} %collective-permute-done.2), channel_id=1, source_target_pairs={{0,4},{4,8},{8,12},{12,16},{16,20},{20,24},{24,28},{28,0},{1,5},{5... | collective-permute-start | bytes 393224 | tf_op jit(solution)/shard_map/ppermute | solution.py:14
  46.2 7.2 %collective-permute-start.6 = (bf16[512,128]{1,0:T(8,128)(2,1)S(1)}, bf16[512,128]{1,0:T(8,128)(2,1)S(1)}, u32[]{:S(2)}, u32[]{:S(2)}) collective-permute-start(bf16[512,128]{1,0:T(8,128)(2,1)S(1)} %collective-permute-done.5), channel_id=1, source_target_pairs={{0,28},{4,0},{8,4},{12,8},{16,12},{20,16},{24,20},{28,24},{1,29},{... | collective-permute-start | bytes 393224 | tf_op jit(solution)/shard_map/ppermute | solution.py:16
  70.8 1.4 copy-start.1
  70.8 1.4 copy-start.2
  81.7 1.4 copy-start.1
  81.7 1.4 copy-start.2
  106.4 10.5 %copy-start = (f32[2,512,4096]{2,1,0:T(8,128)S(1)}, f32[2,512,4096]{2,1,0:T(8,128)}, u32[]{:S(2)}) copy-start(f32[2,512,4096]{2,1,0:T(8,128)} %get-tuple-element.457) | copy-start | bytes 50331652 | tf_op jit(solution)/shard_map/while
  106.4 10.5 %copy-start.5 = (bf16[2,512,128]{2,1,0:T(8,128)(2,1)S(1)}, bf16[2,512,128]{2,1,0:T(8,128)(2,1)}, u32[]{:S(2)}) copy-start(bf16[2,512,128]{2,1,0:T(8,128)(2,1)} %get-tuple-element.443) | copy-start | bytes 786436 | tf_op jit(solution)/shard_map/while
  117.0 6.2 %copy-start.3 = (bf16[2,512,128]{2,1,0:T(8,128)(2,1)S(1)}, bf16[2,512,128]{2,1,0:T(8,128)(2,1)}, u32[]{:S(2)}) copy-start(bf16[2,512,128]{2,1,0:T(8,128)(2,1)} %get-tuple-element.462) | copy-start | bytes 786436 | tf_op jit(solution)/shard_map/while
  122.5 0.7 copy-start.6
  126.8 10.5 %copy-start = (f32[2,512,4096]{2,1,0:T(8,128)S(1)}, f32[2,512,4096]{2,1,0:T(8,128)}, u32[]{:S(2)}) copy-start(f32[2,512,4096]{2,1,0:T(8,128)} %get-tuple-element.457) | copy-start | bytes 50331652 | tf_op jit(solution)/shard_map/while
  126.8 10.5 %copy-start.5 = (bf16[2,512,128]{2,1,0:T(8,128)(2,1)S(1)}, bf16[2,512,128]{2,1,0:T(8,128)(2,1)}, u32[]{:S(2)}) copy-start(bf16[2,512,128]{2,1,0:T(8,128)(2,1)} %get-tuple-element.443) | copy-start | bytes 786436 | tf_op jit(solution)/shard_map/while
  137.3 6.2 %copy-start.3 = (bf16[2,512,128]{2,1,0:T(8,128)(2,1)S(1)}, bf16[2,512,128]{2,1,0:T(8,128)(2,1)}, u32[]{:S(2)}) copy-start(bf16[2,512,128]{2,1,0:T(8,128)(2,1)} %get-tuple-element.462) | copy-start | bytes 786436 | tf_op jit(solution)/shard_map/while
  142.8 0.7 copy-start.6
  148.7 82.2 %reduce-scatter.5.cloned.1.call-start = ((), (), s32[]{:S(2)}) async-start(), calls=%async_computation.4 | async-start | bytes 2359296 | tf_op jit(solution)/shard_map/reduce_scatter | solution.py:121
Sparse Core Ops, SparseCore 0:
  27.3 42.0 all-gather.3
  148.8 10.4 reduce-scatter.2
  163.3 67.6 reduce-scatter.4
